TPU v7x, 32 devices: a whole 2x2x4 slice. The times are simulated.
32 devices in a mesh: rows: 8 (over y, x, core), blk: 4 (over z).
Axes of the slice: x: 2, y: 2, z: 4, core: 2. Of those that a mesh axis runs over, the one named last changes fastest.
Arguments:
- vectors: float32 [6144, 128], P('blk'), may hold values from -6 to 6
- left_intersection: float32 [256, 128, 128], P(('rows', 'blk')), may hold values from -0.5 to 0.5
- right_intersection: float32 [48, 128, 128], P('blk'), may hold values from -0.5 to 0.5
- tiles: float32 [512, 128, 128], P('rows'), may hold values from -0.09375 to 0.09375
- pair_cols: int32 [256, 32], P(('rows', 'blk')), may hold values from 0 to 47, all different within a row
- pair_owner: int32 [256, 32], P(('rows', 'blk')), may hold values from 0 to 7, as said below
- pair_slot: int32 [256, 32], P(('rows', 'blk')), may hold values from 0 to 63
- pair_counts: int32 [256], P(('rows', 'blk')), may hold values from 1 to 32, as said below
Outputs:
- product: float32 [32768, 128], P(('rows', 'blk'))
Inputs may be any that keep to these rules, and one draw needn't show every extreme that they name: `pair_owner`: among the 256 entries of each aligned block of 8 row blocks, every rows index appears exactly 32 times. `pair_cols`: the column blocks listed for one row block are distinct. `pair_counts`: some row block has all 32 entries live.
All inputs are finite; a program needn't handle non-finite values.
Results may differ from a plain program's by a relative error of at most 0.0003.
Values sent between devices are 32-bit elements; how exact they have to be, the bound alone decides.
No kernel may reach another device: no remote copies, remote signals or barrier semaphores. Data moves between devices by JAX's collectives and lax.ppermute only.
A program may use at most 128 MiB of HBM per device.

v0:
```python
import jax
import jax.numpy as jnp
from jax import lax
from jax.sharding import PartitionSpec as P


def pick_rows(table, row_ids, table_rows):
    onehot = (row_ids[:, None] == jnp.arange(table_rows)[None, :]).astype(jnp.float32)
    flat = table.reshape(table_rows, -1)
    picked = jnp.dot(
        onehot, flat, precision=lax.Precision.HIGHEST, preferred_element_type=jnp.float32
    )
    return picked.reshape((row_ids.shape[0],) + table.shape[1:])


def invert_slots(values, slot_index):
    count = slot_index.shape[0]
    matches = slot_index[None, :] == jnp.arange(count)[:, None]
    return jnp.sum(jnp.where(matches, values[None, :], 0), axis=1)


def per_device(
    vectors,
    left_intersection,
    right_intersection,
    tiles,
    pair_cols,
    pair_owner,
    pair_slot,
    pair_counts,
):
    row_blocks, fine_rows, coarse = left_intersection.shape
    listed = pair_cols.shape[1]
    vec_count = vectors.shape[1]
    owners = lax.axis_size("rows")
    entries = row_blocks * listed
    per_owner = entries // owners
    highest = lax.Precision.HIGHEST
    held_tiles = tiles.shape[0]
    flat_owner = pair_owner.reshape(entries)
    earlier = jnp.arange(entries)[:, None] > jnp.arange(entries)[None, :]
    matches = flat_owner[:, None] == flat_owner[None, :]
    position = jnp.sum(jnp.where(matches & earlier, 1, 0), axis=1).astype(jnp.int32)
    slot_index = flat_owner * per_owner + position
    local_blocks = vectors.reshape(right_intersection.shape[0], fine_rows, vec_count)
    entry_ids = jnp.arange(entries)
    block_ids = entry_ids // listed
    count_each = jnp.repeat(pair_counts, listed)
    live_flags = (entry_ids % listed < count_each).astype(jnp.int32)
    block_range = jnp.arange(row_blocks)
    slot_req = invert_slots(pair_slot.reshape(entries), slot_index)
    col_req = invert_slots(pair_cols.reshape(entries), slot_index)
    block_req = invert_slots(block_ids, slot_index)
    live_req = invert_slots(live_flags, slot_index)
    stacked = jnp.stack([slot_req, col_req, block_req, live_req]).reshape(4, owners, per_owner)
    received = lax.all_to_all(stacked, "rows", split_axis=1, concat_axis=1, tiled=True)
    local_proj = jnp.einsum("csu,csv->cuv", right_intersection, local_blocks, precision=highest)
    proj_all = lax.all_gather(local_proj, "blk", axis=0, tiled=True)
    col_total = proj_all.shape[0]

    def per_source(packed):
        slots_here, cols_here, blocks_here, live_here = packed
        chosen = pick_rows(tiles, slots_here, held_tiles)
        picked = pick_rows(proj_all, cols_here, col_total)
        applied = jnp.einsum("ptu,puv->ptv", chosen, picked, precision=highest)
        weights = (
            (blocks_here[None, :] == block_range[:, None]) & (live_here[None, :] > 0)
        ).astype(jnp.float32)
        return jnp.einsum("rp,ptv->rtv", weights, applied, precision=highest)

    partial_sums = lax.map(per_source, (received[0], received[1], received[2], received[3]))
    returned = lax.all_to_all(partial_sums, "rows", split_axis=0, concat_axis=0, tiled=True)
    summed = jnp.sum(returned, axis=0)
    result = jnp.einsum("bft,btv->bfv", left_intersection, summed, precision=highest)
    return result.reshape(row_blocks * fine_rows, vec_count)


def solution(mesh):
    return jax.shard_map(
        per_device,
        mesh=mesh,
        in_specs=(
            P("blk", None),
            P(("rows", "blk"), None, None),
            P("blk", None, None),
            P("rows", None, None),
            P(("rows", "blk"), None),
            P(("rows", "blk"), None),
            P(("rows", "blk"), None),
            P(("rows", "blk")),
        ),
        out_specs=P(("rows", "blk"), None),
        check_vma=False,
    )
```

profile of v0, /device:TPU:0, one launch (start us, length us, event | category | flops | bytes accessed | tf_op | source)
XLA Modules:
  0.0 277.5 jit_solution(6628994686971753800)
XLA Ops:
  6.5 0.0 copy-start
  6.5 0.0 all-gather.2.cloned.1.call-start
  6.6 1.1 copy-done
  7.7 3.4 %fusion.40 = f32[12,128,128]{2,1,0:T(8,128)} fusion(f32[12,128,128]{2,1,0:T(8,128)} %param.12, f32[12,128,128]{2,1,0:T(8,128)S(1)} %bitcast.91), kind=kOutput, calls=%fused_computation.57 | convolution fusion | flops 301989888 | bytes 2359296 | tf_op jit(solution)/shard_map/csu,csv->cuv/dot_general | solution.py:57
  11.1 0.0 all-gather.2.cloned.1.call-update
  11.1 0.0 copy-done.3
  11.1 0.1 reshape.76
  11.2 0.0 copy-done.6
  11.2 0.1 broadcast_in_dim.77
  11.3 0.1 reshape.77
  11.4 0.0 copy-done.4
  11.4 0.1 broadcast_in_dim.72
  11.5 0.0 copy-done.5
  11.5 0.1 broadcast_in_dim.74
  11.5 0.2 select_reduce_fusion.4
  11.7 0.2 select_reduce_fusion.3
  12.0 0.1 stack.15
  12.1 0.1 stack.16
  12.1 0.1 stack.17
  12.2 0.1 stack.18
  12.3 0.7 reshape.85
  13.0 5.2 %all-to-all-start = ((s32[8,1,128]{2,1,0:T(1,128)}), s32[8,1,128]{2,1,0:T(1,128)S(1)}, u32[]{:S(2)}, u32[]{:S(2)}) async-start(s32[8,1,128]{2,1,0:T(1,128)} %reshape.85), calls=%async_computation | async-start | bytes 8192 | tf_op jit(solution)/shard_map/all_to_all | solution.py:56
  18.2 4.6 %all-to-all-done = s32[8,1,128]{2,1,0:T(1,128)S(1)} async-done(((s32[8,1,128]{2,1,0:T(1,128)}), s32[8,1,128]{2,1,0:T(1,128)S(1)}, u32[]{:S(2)}, u32[]{:S(2)}) %all-to-all-start) | async-done | bytes 4128 | tf_op jit(solution)/shard_map/all_to_all | solution.py:56
  22.8 0.5 broadcast.64
  23.3 0.7 reduce
  24.0 0.1 reshape.86
  24.1 53.3 %all-gather.2.cloned.1.call-done = f32[48,128,128]{2,1,0:T(8,128)} async-done(((f32[12,128,128]{2,1,0:T(8,128)}), f32[48,128,128]{2,1,0:T(8,128)}) %all-gather.2.cloned.1.call-update) | async-done | bytes 3145744 | tf_op jit(solution)/shard_map/all_gather | solution.py:58
  77.5 135.7 %while.11 = (s32[]{:T(128)}, f32[8,8,128,128]{3,1,2,0:T(8,128)}, s32[8,32]{1,0:T(8,128)S(1)}, s32[8,32]{1,0:T(8,128)S(1)}, s32[8,32]{1,0:T(8,128)S(1)}, /*index=...) while((s32[]{:T(128)}, f32[8,8,128,128]{3,1,2,0:T(8,128)}, ...), condition=%wide.region_6.7_spmd.clone, body=%wide.region_5.6_spmd.clone.sunk | while | flops 1560285184 | bytes 33032132 | solution.py:71
  77.5 6.2 %fusion.69 = f32[32,128,128]{2,0,1:T(8,128)S(1)} fusion(s32[32]{0:T(128)S(1)} %get-tuple-element.150, f32[8,8,128,128]{3,2,1,0:T(8,128)} %bitcast.92), kind=kOutput, calls=%fused_computation.2.clone.1 | convolution fusion | flops 402655232 | bytes 6291584 | tf_op jit(solution)/shard_map/while/body/eval_jaxpr/dot_general | solution.py:10
  83.7 3.3 %fusion.67 = f32[32,128,128]{2,0,1:T(8,128)S(1)} fusion(s32[32]{0:T(128)S(1)} %fusion.66, f32[6,8,128,128]{3,2,1,0:T(8,128)S(1)} %bitcast.93), kind=kOutput, calls=%fused_computation.6.clone.1 | convolution fusion | flops 301991424 | bytes 5243008 | tf_op jit(solution)/shard_map/while/body/eval_jaxpr/dot_general | solution.py:10
  87.0 4.6 %fusion.70 = f32[32,128,128]{2,1,0:T(8,128)S(1)} fusion(f32[32,128,128]{2,0,1:T(8,128)S(1)} %fusion.67, f32[32,128,128]{2,0,1:T(8,128)S(1)} %fusion.69), kind=kOutput, calls=%fused_computation.11.clone.1 | convolution fusion | flops 805306368 | bytes 6291456 | tf_op jit(solution)/shard_map/while/body/eval_jaxpr/ptu,puv->ptv/dot_general | solution.py:65
  91.6 2.8 fusion.71
  94.4 6.2 %fusion.69 = f32[32,128,128]{2,0,1:T(8,128)S(1)} fusion(s32[32]{0:T(128)S(1)} %get-tuple-element.150, f32[8,8,128,128]{3,2,1,0:T(8,128)} %bitcast.92), kind=kOutput, calls=%fused_computation.2.clone.1 | convolution fusion | flops 402655232 | bytes 6291584 | tf_op jit(solution)/shard_map/while/body/eval_jaxpr/dot_general | solution.py:10
  100.6 3.3 %fusion.67 = f32[32,128,128]{2,0,1:T(8,128)S(1)} fusion(s32[32]{0:T(128)S(1)} %fusion.66, f32[6,8,128,128]{3,2,1,0:T(8,128)S(1)} %bitcast.93), kind=kOutput, calls=%fused_computation.6.clone.1 | convolution fusion | flops 301991424 | bytes 5243008 | tf_op jit(solution)/shard_map/while/body/eval_jaxpr/dot_general | solution.py:10
  104.0 4.6 %fusion.70 = f32[32,128,128]{2,1,0:T(8,128)S(1)} fusion(f32[32,128,128]{2,0,1:T(8,128)S(1)} %fusion.67, f32[32,128,128]{2,0,1:T(8,128)S(1)} %fusion.69), kind=kOutput, calls=%fused_computation.11.clone.1 | convolution fusion | flops 805306368 | bytes 6291456 | tf_op jit(solution)/shard_map/while/body/eval_jaxpr/ptu,puv->ptv/dot_general | solution.py:65
  108.6 2.8 %fusion.71 = f32[8,8,128,128]{3,1,2,0:T(8,128)} fusion(f32[8,8,128,128]{3,1,2,0:T(8,128)} %get-tuple-element.162, s32[]{:T(128)} %get-tuple-element.161, f32[32,128,128]{2,1,0:T(8,128)S(1)} %fusion.70, s32[32]{0:T(128)S(1)} %get-tuple-element.151, pred[32]{0:T(512)(128)(4,1)S(1)} %compare_bitcast_fusion.2), kind=kOutput, calls=%fused_computation.15.clone.1 | convolution fusion | flops 50332160 | bytes 2622112 | tf_op jit(solution)/shard_map/while/body/eval_jaxpr/rp,ptv->rtv/dot_general | solution.py:69
  111.4 6.2 %fusion.69 = f32[32,128,128]{2,0,1:T(8,128)S(1)} fusion(s32[32]{0:T(128)S(1)} %get-tuple-element.150, f32[8,8,128,128]{3,2,1,0:T(8,128)} %bitcast.92), kind=kOutput, calls=%fused_computation.2.clone.1 | convolution fusion | flops 402655232 | bytes 6291584 | tf_op jit(solution)/shard_map/while/body/eval_jaxpr/dot_general | solution.py:10
  117.6 3.3 %fusion.67 = f32[32,128,128]{2,0,1:T(8,128)S(1)} fusion(s32[32]{0:T(128)S(1)} %fusion.66, f32[6,8,128,128]{3,2,1,0:T(8,128)S(1)} %bitcast.93), kind=kOutput, calls=%fused_computation.6.clone.1 | convolution fusion | flops 301991424 | bytes 5243008 | tf_op jit(solution)/shard_map/while/body/eval_jaxpr/dot_general | solution.py:10
  120.9 4.6 %fusion.70 = f32[32,128,128]{2,1,0:T(8,128)S(1)} fusion(f32[32,128,128]{2,0,1:T(8,128)S(1)} %fusion.67, f32[32,128,128]{2,0,1:T(8,128)S(1)} %fusion.69), kind=kOutput, calls=%fused_computation.11.clone.1 | convolution fusion | flops 805306368 | bytes 6291456 | tf_op jit(solution)/shard_map/while/body/eval_jaxpr/ptu,puv->ptv/dot_general | solution.py:65
  125.5 2.8 %fusion.71 = f32[8,8,128,128]{3,1,2,0:T(8,128)} fusion(f32[8,8,128,128]{3,1,2,0:T(8,128)} %get-tuple-element.162, s32[]{:T(128)} %get-tuple-element.161, f32[32,128,128]{2,1,0:T(8,128)S(1)} %fusion.70, s32[32]{0:T(128)S(1)} %get-tuple-element.151, pred[32]{0:T(512)(128)(4,1)S(1)} %compare_bitcast_fusion.2), kind=kOutput, calls=%fused_computation.15.clone.1 | convolution fusion | flops 50332160 | bytes 2622112 | tf_op jit(solution)/shard_map/while/body/eval_jaxpr/rp,ptv->rtv/dot_general | solution.py:69
  128.3 6.2 %fusion.69 = f32[32,128,128]{2,0,1:T(8,128)S(1)} fusion(s32[32]{0:T(128)S(1)} %get-tuple-element.150, f32[8,8,128,128]{3,2,1,0:T(8,128)} %bitcast.92), kind=kOutput, calls=%fused_computation.2.clone.1 | convolution fusion | flops 402655232 | bytes 6291584 | tf_op jit(solution)/shard_map/while/body/eval_jaxpr/dot_general | solution.py:10
  134.6 3.3 %fusion.67 = f32[32,128,128]{2,0,1:T(8,128)S(1)} fusion(s32[32]{0:T(128)S(1)} %fusion.66, f32[6,8,128,128]{3,2,1,0:T(8,128)S(1)} %bitcast.93), kind=kOutput, calls=%fused_computation.6.clone.1 | convolution fusion | flops 301991424 | bytes 5243008 | tf_op jit(solution)/shard_map/while/body/eval_jaxpr/dot_general | solution.py:10
  137.9 4.6 %fusion.70 = f32[32,128,128]{2,1,0:T(8,128)S(1)} fusion(f32[32,128,128]{2,0,1:T(8,128)S(1)} %fusion.67, f32[32,128,128]{2,0,1:T(8,128)S(1)} %fusion.69), kind=kOutput, calls=%fused_computation.11.clone.1 | convolution fusion | flops 805306368 | bytes 6291456 | tf_op jit(solution)/shard_map/while/body/eval_jaxpr/ptu,puv->ptv/dot_general | solution.py:65
  142.5 2.8 %fusion.71 = f32[8,8,128,128]{3,1,2,0:T(8,128)} fusion(f32[8,8,128,128]{3,1,2,0:T(8,128)} %get-tuple-element.162, s32[]{:T(128)} %get-tuple-element.161, f32[32,128,128]{2,1,0:T(8,128)S(1)} %fusion.70, s32[32]{0:T(128)S(1)} %get-tuple-element.151, pred[32]{0:T(512)(128)(4,1)S(1)} %compare_bitcast_fusion.2), kind=kOutput, calls=%fused_computation.15.clone.1 | convolution fusion | flops 50332160 | bytes 2622112 | tf_op jit(solution)/shard_map/while/body/eval_jaxpr/rp,ptv->rtv/dot_general | solution.py:69
  145.3 6.2 %fusion.69 = f32[32,128,128]{2,0,1:T(8,128)S(1)} fusion(s32[32]{0:T(128)S(1)} %get-tuple-element.150, f32[8,8,128,128]{3,2,1,0:T(8,128)} %bitcast.92), kind=kOutput, calls=%fused_computation.2.clone.1 | convolution fusion | flops 402655232 | bytes 6291584 | tf_op jit(solution)/shard_map/while/body/eval_jaxpr/dot_general | solution.py:10
  151.5 3.3 %fusion.67 = f32[32,128,128]{2,0,1:T(8,128)S(1)} fusion(s32[32]{0:T(128)S(1)} %fusion.66, f32[6,8,128,128]{3,2,1,0:T(8,128)S(1)} %bitcast.93), kind=kOutput, calls=%fused_computation.6.clone.1 | convolution fusion | flops 301991424 | bytes 5243008 | tf_op jit(solution)/shard_map/while/body/eval_jaxpr/dot_general | solution.py:10
  154.9 4.6 %fusion.70 = f32[32,128,128]{2,1,0:T(8,128)S(1)} fusion(f32[32,128,128]{2,0,1:T(8,128)S(1)} %fusion.67, f32[32,128,128]{2,0,1:T(8,128)S(1)} %fusion.69), kind=kOutput, calls=%fused_computation.11.clone.1 | convolution fusion | flops 805306368 | bytes 6291456 | tf_op jit(solution)/shard_map/while/body/eval_jaxpr/ptu,puv->ptv/dot_general | solution.py:65
  159.5 2.8 fusion.71
  162.2 6.2 %fusion.69 = f32[32,128,128]{2,0,1:T(8,128)S(1)} fusion(s32[32]{0:T(128)S(1)} %get-tuple-element.150, f32[8,8,128,128]{3,2,1,0:T(8,128)} %bitcast.92), kind=kOutput, calls=%fused_computation.2.clone.1 | convolution fusion | flops 402655232 | bytes 6291584 | tf_op jit(solution)/shard_map/while/body/eval_jaxpr/dot_general | solution.py:10
  168.5 3.3 %fusion.67 = f32[32,128,128]{2,0,1:T(8,128)S(1)} fusion(s32[32]{0:T(128)S(1)} %fusion.66, f32[6,8,128,128]{3,2,1,0:T(8,128)S(1)} %bitcast.93), kind=kOutput, calls=%fused_computation.6.clone.1 | convolution fusion | flops 301991424 | bytes 5243008 | tf_op jit(solution)/shard_map/while/body/eval_jaxpr/dot_general | solution.py:10
  171.8 4.6 %fusion.70 = f32[32,128,128]{2,1,0:T(8,128)S(1)} fusion(f32[32,128,128]{2,0,1:T(8,128)S(1)} %fusion.67, f32[32,128,128]{2,0,1:T(8,128)S(1)} %fusion.69), kind=kOutput, calls=%fused_computation.11.clone.1 | convolution fusion | flops 805306368 | bytes 6291456 | tf_op jit(solution)/shard_map/while/body/eval_jaxpr/ptu,puv->ptv/dot_general | solution.py:65
  176.4 2.8 %fusion.71 = f32[8,8,128,128]{3,1,2,0:T(8,128)} fusion(f32[8,8,128,128]{3,1,2,0:T(8,128)} %get-tuple-element.162, s32[]{:T(128)} %get-tuple-element.161, f32[32,128,128]{2,1,0:T(8,128)S(1)} %fusion.70, s32[32]{0:T(128)S(1)} %get-tuple-element.151, pred[32]{0:T(512)(128)(4,1)S(1)} %compare_bitcast_fusion.2), kind=kOutput, calls=%fused_computation.15.clone.1 | convolution fusion | flops 50332160 | bytes 2622112 | tf_op jit(solution)/shard_map/while/body/eval_jaxpr/rp,ptv->rtv/dot_general | solution.py:69
  179.2 6.2 %fusion.69 = f32[32,128,128]{2,0,1:T(8,128)S(1)} fusion(s32[32]{0:T(128)S(1)} %get-tuple-element.150, f32[8,8,128,128]{3,2,1,0:T(8,128)} %bitcast.92), kind=kOutput, calls=%fused_computation.2.clone.1 | convolution fusion | flops 402655232 | bytes 6291584 | tf_op jit(solution)/shard_map/while/body/eval_jaxpr/dot_general | solution.py:10
  185.4 0.0 copy-done.1
  185.5 3.3 %fusion.67 = f32[32,128,128]{2,0,1:T(8,128)S(1)} fusion(s32[32]{0:T(128)S(1)} %fusion.66, f32[6,8,128,128]{3,2,1,0:T(8,128)S(1)} %bitcast.93), kind=kOutput, calls=%fused_computation.6.clone.1 | convolution fusion | flops 301991424 | bytes 5243008 | tf_op jit(solution)/shard_map/while/body/eval_jaxpr/dot_general | solution.py:10
  188.8 4.6 %fusion.70 = f32[32,128,128]{2,1,0:T(8,128)S(1)} fusion(f32[32,128,128]{2,0,1:T(8,128)S(1)} %fusion.67, f32[32,128,128]{2,0,1:T(8,128)S(1)} %fusion.69), kind=kOutput, calls=%fused_computation.11.clone.1 | convolution fusion | flops 805306368 | bytes 6291456 | tf_op jit(solution)/shard_map/while/body/eval_jaxpr/ptu,puv->ptv/dot_general | solution.py:65
  193.4 2.8 fusion.71
  196.1 6.2 %fusion.69 = f32[32,128,128]{2,0,1:T(8,128)S(1)} fusion(s32[32]{0:T(128)S(1)} %get-tuple-element.150, f32[8,8,128,128]{3,2,1,0:T(8,128)} %bitcast.92), kind=kOutput, calls=%fused_computation.2.clone.1 | convolution fusion | flops 402655232 | bytes 6291584 | tf_op jit(solution)/shard_map/while/body/eval_jaxpr/dot_general | solution.py:10
  202.4 3.3 %fusion.67 = f32[32,128,128]{2,0,1:T(8,128)S(1)} fusion(s32[32]{0:T(128)S(1)} %fusion.66, f32[6,8,128,128]{3,2,1,0:T(8,128)S(1)} %bitcast.93), kind=kOutput, calls=%fused_computation.6.clone.1 | convolution fusion | flops 301991424 | bytes 5243008 | tf_op jit(solution)/shard_map/while/body/eval_jaxpr/dot_general | solution.py:10
  205.7 4.6 %fusion.70 = f32[32,128,128]{2,1,0:T(8,128)S(1)} fusion(f32[32,128,128]{2,0,1:T(8,128)S(1)} %fusion.67, f32[32,128,128]{2,0,1:T(8,128)S(1)} %fusion.69), kind=kOutput, calls=%fused_computation.11.clone.1 | convolution fusion | flops 805306368 | bytes 6291456 | tf_op jit(solution)/shard_map/while/body/eval_jaxpr/ptu,puv->ptv/dot_general | solution.py:65
  210.3 2.8 %fusion.71 = f32[8,8,128,128]{3,1,2,0:T(8,128)} fusion(f32[8,8,128,128]{3,1,2,0:T(8,128)} %get-tuple-element.162, s32[]{:T(128)} %get-tuple-element.161, f32[32,128,128]{2,1,0:T(8,128)S(1)} %fusion.70, s32[32]{0:T(128)S(1)} %get-tuple-element.151, pred[32]{0:T(512)(128)(4,1)S(1)} %compare_bitcast_fusion.2), kind=kOutput, calls=%fused_computation.15.clone.1 | convolution fusion | flops 50332160 | bytes 2622112 | tf_op jit(solution)/shard_map/while/body/eval_jaxpr/rp,ptv->rtv/dot_general | solution.py:69
  213.1 53.5 %all_to_all.10 = f32[8,8,128,128]{3,1,2,0:T(8,128)} all-to-all(f32[8,8,128,128]{3,1,2,0:T(8,128)} %get-tuple-element.52), channel_id=1, replica_groups=mesh['rows'=8,'blk'=4] {'rows'}, dimensions={0} | all-to-all | bytes 8388608 | tf_op jit(solution)/shard_map/all_to_all | solution.py:72
  266.6 2.5 reduce_sum.59
  269.1 1.5 fusion.33
  (50 shorter events, 0.3 us)
Async XLA Ops:
  6.5 1.1 copy-start
  6.5 4.6 %copy-start.3 = (s32[8,32]{1,0:T(8,128)S(1)}, s32[8,32]{1,0:T(8,128)}, u32[]{:S(2)}) copy-start(s32[8,32]{1,0:T(8,128)} %param.15) | copy-start | bytes 3076
  6.5 4.7 %copy-start.6 = (s32[8]{0:T(128)S(1)}, s32[8]{0:T(128)}, u32[]{:S(2)}) copy-start(s32[8]{0:T(128)} %param.17) | copy-start | bytes 100
  6.5 4.8 %copy-start.4 = (s32[8,32]{1,0:T(8,128)S(1)}, s32[8,32]{1,0:T(8,128)}, u32[]{:S(2)}) copy-start(s32[8,32]{1,0:T(8,128)} %param.16) | copy-start | bytes 3076
  6.5 4.9 %copy-start.5 = (s32[8,32]{1,0:T(8,128)S(1)}, s32[8,32]{1,0:T(8,128)}, u32[]{:S(2)}) copy-start(s32[8,32]{1,0:T(8,128)} %param.14) | copy-start | bytes 3076
  6.5 70.9 %all-gather.2.cloned.1.call-start = ((), (), s32[]{:S(2)}) async-start(), calls=%async_computation.2 | async-start | bytes 3932160 | tf_op jit(solution)/shard_map/all_gather | solution.py:58
  13.0 9.8 %all-to-all-start = ((s32[8,1,128]{2,1,0:T(1,128)}), s32[8,1,128]{2,1,0:T(1,128)S(1)}, u32[]{:S(2)}, u32[]{:S(2)}) async-start(s32[8,1,128]{2,1,0:T(1,128)} %reshape.85), calls=%async_computation | async-start | bytes 8192 | tf_op jit(solution)/shard_map/all_to_all | solution.py:56
  77.5 6.2 %copy-start.1 = (f32[48,128,128]{2,1,0:T(8,128)S(1)}, f32[48,128,128]{2,1,0:T(8,128)}, u32[]{:S(2)}) copy-start(f32[48,128,128]{2,1,0:T(8,128)} %get-tuple-element.177) | copy-start | bytes 9437188 | tf_op jit(solution)/shard_map/while
  94.4 6.2 %copy-start.1 = (f32[48,128,128]{2,1,0:T(8,128)S(1)}, f32[48,128,128]{2,1,0:T(8,128)}, u32[]{:S(2)}) copy-start(f32[48,128,128]{2,1,0:T(8,128)} %get-tuple-element.177) | copy-start | bytes 9437188 | tf_op jit(solution)/shard_map/while
  111.4 6.2 %copy-start.1 = (f32[48,128,128]{2,1,0:T(8,128)S(1)}, f32[48,128,128]{2,1,0:T(8,128)}, u32[]{:S(2)}) copy-start(f32[48,128,128]{2,1,0:T(8,128)} %get-tuple-element.177) | copy-start | bytes 9437188 | tf_op jit(solution)/shard_map/while
  128.3 6.2 %copy-start.1 = (f32[48,128,128]{2,1,0:T(8,128)S(1)}, f32[48,128,128]{2,1,0:T(8,128)}, u32[]{:S(2)}) copy-start(f32[48,128,128]{2,1,0:T(8,128)} %get-tuple-element.177) | copy-start | bytes 9437188 | tf_op jit(solution)/shard_map/while
  145.3 6.2 %copy-start.1 = (f32[48,128,128]{2,1,0:T(8,128)S(1)}, f32[48,128,128]{2,1,0:T(8,128)}, u32[]{:S(2)}) copy-start(f32[48,128,128]{2,1,0:T(8,128)} %get-tuple-element.177) | copy-start | bytes 9437188 | tf_op jit(solution)/shard_map/while
  162.2 6.2 %copy-start.1 = (f32[48,128,128]{2,1,0:T(8,128)S(1)}, f32[48,128,128]{2,1,0:T(8,128)}, u32[]{:S(2)}) copy-start(f32[48,128,128]{2,1,0:T(8,128)} %get-tuple-element.177) | copy-start | bytes 9437188 | tf_op jit(solution)/shard_map/while
  179.2 6.2 %copy-start.1 = (f32[48,128,128]{2,1,0:T(8,128)S(1)}, f32[48,128,128]{2,1,0:T(8,128)}, u32[]{:S(2)}) copy-start(f32[48,128,128]{2,1,0:T(8,128)} %get-tuple-element.177) | copy-start | bytes 9437188 | tf_op jit(solution)/shard_map/while
  196.1 6.2 %copy-start.1 = (f32[48,128,128]{2,1,0:T(8,128)S(1)}, f32[48,128,128]{2,1,0:T(8,128)}, u32[]{:S(2)}) copy-start(f32[48,128,128]{2,1,0:T(8,128)} %get-tuple-element.177) | copy-start | bytes 9437188 | tf_op jit(solution)/shard_map/while
  266.6 2.5 copy-start.2
Sparse Core Ops, SparseCore 0:
  11.2 66.1 all-gather.1
where the time goes:
time: 278 us; the launch traced here: 277 us
  matrix products  140 us (50%)
  waiting for transfers between devices  58 us (21%)
  blocking collectives  53.5 us (19%)
  between operations  13.5 us (5%)
  starting transfers between devices  5.24 us (2%)
  other arithmetic  3.71 us (1%)
  local copies, waits for them, and re-layouts  3.25 us (1%)
    dot_general x16, matrix products, pick_rows(): jnp.dot(onehot, flat, precision=lax.Precision.HIGHEST, preferred_element_...  76.3 us
    all_to_all x1, blocking collectives, per_device(): lax.all_to_all(partial_sums, 'rows', split_axis=0, concat_axis=0, tiled=T...  53.5 us
    all_gather x1, waiting for transfers between devices, per_device(): proj_all = lax.all_gather(local_proj, 'blk', axis=0, tiled=True)  53.3 us
    dot_general x8, matrix products, per_source(): applied = jnp.einsum('ptu,puv->ptv', chosen, picked, precision=highest)  36.6 us
    dot_general x8, matrix products, per_source(): return jnp.einsum('rp,ptv->rtv', weights, applied, precision=highest)  22.2 us
  transfers between devices with their start and end apart: 2, of which 2 were waited for; matrix products, arithmetic and copies ran while one was open for 1% of the time, Pallas kernels for 0%

commit v1 on v0

--- a/solution.py
+++ b/solution.py
@@ -2,6 +2,27 @@
 import jax.numpy as jnp
 from jax import lax
 from jax.sharding import PartitionSpec as P
+
+
+def gather_around(x, axis, dim):
+    devices, index, rows = (lax.axis_size(axis), lax.axis_index(axis), x.shape[dim])
+    right = [(i, (i + 1) % devices) for i in range(devices)]
+    downward = [(i, (i - 1) % devices) for i in range(devices)]
+    out = jnp.zeros((*x.shape[:dim], devices * rows, *x.shape[dim + 1 :]), x.dtype)
+    out = lax.dynamic_update_slice_in_dim(out, x, index * rows, axis=dim)
+    from_left = from_right = x
+    middle = devices // 2
+    for turn in range(1, middle + 1):
+        from_left = lax.ppermute(from_left, axis, right)
+        out = lax.dynamic_update_slice_in_dim(
+            out, from_left, (index - turn) % devices * rows, axis=dim
+        )
+        if turn < devices - middle:
+            from_right = lax.ppermute(from_right, axis, downward)
+            out = lax.dynamic_update_slice_in_dim(
+                out, from_right, (index + turn) % devices * rows, axis=dim
+            )
+    return out
 
 
 def pick_rows(table, row_ids, table_rows):
@@ -55,7 +76,7 @@
     stacked = jnp.stack([slot_req, col_req, block_req, live_req]).reshape(4, owners, per_owner)
     received = lax.all_to_all(stacked, "rows", split_axis=1, concat_axis=1, tiled=True)
     local_proj = jnp.einsum("csu,csv->cuv", right_intersection, local_blocks, precision=highest)
-    proj_all = lax.all_gather(local_proj, "blk", axis=0, tiled=True)
+    proj_all = gather_around(local_proj, "blk", 0)
     col_total = proj_all.shape[0]
 
     def per_source(packed):

time: 278 us -> 269 us (0.968)
  waiting for transfers between devices: 58 us -> 42.5 us
  between operations: 13.5 us -> 0.07 us
  matrix products: 140 us -> 151 us
  local copies, waits for them, and re-layouts: 3.25 us -> 8.19 us
  starting transfers between devices: 5.24 us -> 9.03 us
    all_gather x1 -> x0, waiting for transfers between devices: 53.3 us -> none  [per_device(): proj_all = lax.all_gather(local_proj, 'blk', axis=0, tiled=True)]
    ppermute x0 -> x3, waiting for transfers between devices: none -> 37.8 us  [the longest x2 34.4 us: gather_around(): from_left = lax.ppermute(from_left, axis, right)]
    dot_general x16, matrix products: 76.3 us -> 88.6 us  [pick_rows(): jnp.dot(onehot, flat, precision=lax.Precision.HIGHEST, preferred_element_...]
    ppermute x0 -> x3, starting transfers between devices: none -> 5.07 us  [the longest x2 3.06 us: gather_around(): from_left = lax.ppermute(from_left, axis, right)]
    dynamic_update_slice x0 -> x3, local copies, waits for them, and re-layouts: none -> 2.85 us  [the longest x2 1.9 us: gather_around(): lax.dynamic_update_slice_in_dim(out, from_left, (index - turn) % devices...]
  transfers between devices with their start and end apart: 2 -> 4, of which waited for: 2 -> 4; matrix products, arithmetic and copies ran while one was open for 1% -> 2% of each run, Pallas kernels for 0% -> 0%
where the time goes in v1:
time: 269 us
  matrix products  151 us (56%)
  blocking collectives  53.5 us (20%)
  waiting for transfers between devices  42.5 us (16%)
  starting transfers between devices  9.03 us (3%)
  local copies, waits for them, and re-layouts  8.19 us (3%)
  other arithmetic  3.71 us (1%)
    dot_general x16, matrix products, pick_rows(): jnp.dot(onehot, flat, precision=lax.Precision.HIGHEST, preferred_element_...  88.6 us
    all_to_all x1, blocking collectives, per_device(): lax.all_to_all(partial_sums, 'rows', split_axis=0, concat_axis=0, tiled=T...  53.5 us
    dot_general x8, matrix products, per_source(): applied = jnp.einsum('ptu,puv->ptv', chosen, picked, precision=highest)  36.6 us
    ppermute x2, waiting for transfers between devices, gather_around(): from_left = lax.ppermute(from_left, axis, right)  34.4 us
    dot_general x8, matrix products, per_source(): return jnp.einsum('rp,ptv->rtv', weights, applied, precision=highest)  22.2 us
  transfers between devices with their start and end apart: 4, of which 4 were waited for; matrix products, arithmetic and copies ran while one was open for 2% of the time, Pallas kernels for 0%

profile of v1, /device:TPU:0, one launch (start us, length us, event | category | flops | bytes accessed | tf_op | source)
XLA Modules:
  0.0 268.7 jit_solution(16089396058646462645)
XLA Ops:
  0.0 1.1 copy-done
  1.1 2.1 broadcast_in_dim.82
  3.2 2.6 constant_dynamic-update-slice_fusion.3
  5.8 3.1 %collective-permute-start = (f32[12,128,128]{2,1,0:T(8,128)}, f32[12,128,128]{2,1,0:T(8,128)S(1)}, u32[]{:S(2)}, u32[]{:S(2)}) collective-permute-start(f32[12,128,128]{2,1,0:T(8,128)} %get-tuple-element.98), channel_id=1, source_target_pairs={{0,1},{1,2},{2,3},{3,0},{4,5},{5,6},{6,7},{7,4},{8,9},{9,10},{10,1... | collective-permute-start | bytes 2359304 | tf_op jit(solution)/shard_map/ppermute | solution.py:16
  8.9 2.0 collective-permute-start.1
  10.9 0.1 reshape.76
  11.0 0.1 broadcast_in_dim.80
  11.0 0.1 reshape.77
  11.1 0.2 select_reduce_fusion.4
  11.3 18.2 %collective-permute-done = f32[12,128,128]{2,1,0:T(8,128)S(1)} collective-permute-done((f32[12,128,128]{2,1,0:T(8,128)}, f32[12,128,128]{2,1,0:T(8,128)S(1)}, u32[]{:S(2)}, u32[]{:S(2)}) %collective-permute-start) | collective-permute-done | bytes 786464 | tf_op jit(solution)/shard_map/ppermute | solution.py:16
  29.5 0.1 broadcast_in_dim.75
  29.6 0.1 broadcast_in_dim.77
  29.7 0.2 select_reduce_fusion.3
  29.9 0.1 stack.15
  30.0 0.1 stack.16
  30.1 0.1 stack.17
  30.2 0.1 stack.18
  30.3 0.7 reshape.85
  31.0 4.0 %all-to-all-start = ((s32[8,1,128]{2,1,0:T(1,128)}), s32[8,1,128]{2,1,0:T(1,128)S(1)}, u32[]{:S(2)}, u32[]{:S(2)}) async-start(s32[8,1,128]{2,1,0:T(1,128)} %reshape.85), calls=%async_computation | async-start | bytes 8192 | tf_op jit(solution)/shard_map/all_to_all | solution.py:77
  34.9 4.6 %all-to-all-done = s32[8,1,128]{2,1,0:T(1,128)S(1)} async-done(((s32[8,1,128]{2,1,0:T(1,128)}), s32[8,1,128]{2,1,0:T(1,128)S(1)}, u32[]{:S(2)}, u32[]{:S(2)}) %all-to-all-start) | async-done | bytes 4128 | tf_op jit(solution)/shard_map/all_to_all | solution.py:77
  39.5 0.5 broadcast.67
  40.0 0.7 reduce
  40.7 0.1 reshape.86
  40.8 1.0 constant_dynamic-update-slice_fusion.2
  41.8 3.4 %collective-permute-done.1 = f32[12,128,128]{2,1,0:T(8,128)S(1)} collective-permute-done((f32[12,128,128]{2,1,0:T(8,128)}, f32[12,128,128]{2,1,0:T(8,128)S(1)}, u32[]{:S(2)}, u32[]{:S(2)}) %collective-permute-start.1) | collective-permute-done | bytes 786464 | tf_op jit(solution)/shard_map/ppermute | solution.py:21
  45.2 1.0 constant_dynamic-update-slice_fusion.1
  46.1 16.2 %collective-permute-done.2 = f32[12,128,128]{2,1,0:T(8,128)S(1)} collective-permute-done((f32[12,128,128]{2,1,0:T(8,128)S(1)}, f32[12,128,128]{2,1,0:T(8,128)S(1)}, u32[]{:S(2)}, u32[]{:S(2)}) %collective-permute-start.2) | collective-permute-done | bytes 786464 | tf_op jit(solution)/shard_map/ppermute | solution.py:16
  62.4 0.9 constant_dynamic-update-slice_fusion
  63.3 147.8 %while.11 = (s32[]{:T(128)}, f32[8,8,128,128]{3,1,2,0:T(8,128)}, s32[8,32]{1,0:T(8,128)S(1)}, s32[8,32]{1,0:T(8,128)S(1)}, s32[8,32]{1,0:T(8,128)S(1)}, /*index=...) while((s32[]{:T(128)}, f32[8,8,128,128]{3,1,2,0:T(8,128)}, ...), condition=%wide.region_6.7_spmd.clone, body=%wide.region_5.6_spmd.clone.sunk | while | flops 1560285184 | bytes 20449192 | solution.py:92
  63.3 6.1 %fusion.68 = f32[32,128,128]{2,0,1:T(8,128)S(1)} fusion(s32[32]{0:T(128)S(1)} %get-tuple-element.152, f32[8,8,128,128]{3,2,1,0:T(8,128)} %bitcast.92), kind=kOutput, calls=%fused_computation.2.clone.1 | convolution fusion | flops 402655232 | bytes 6291584 | tf_op jit(solution)/shard_map/while/body/eval_jaxpr/dot_general | solution.py:31
  69.4 5.0 %fusion.66 = f32[32,128,128]{2,0,1:T(8,128)S(1)} fusion(s32[32]{0:T(128)S(1)} %fusion.65, f32[6,8,128,128]{3,2,1,0:T(8,128)} %bitcast.89), kind=kOutput, calls=%fused_computation.6.clone.1 | convolution fusion | flops 301991424 | bytes 5243008 | tf_op jit(solution)/shard_map/while/body/eval_jaxpr/dot_general | solution.py:31
  74.4 4.6 %fusion.69 = f32[32,128,128]{2,1,0:T(8,128)S(1)} fusion(f32[32,128,128]{2,0,1:T(8,128)S(1)} %fusion.66, f32[32,128,128]{2,0,1:T(8,128)S(1)} %fusion.68), kind=kOutput, calls=%fused_computation.11.clone.1 | convolution fusion | flops 805306368 | bytes 6291456 | tf_op jit(solution)/shard_map/while/body/eval_jaxpr/ptu,puv->ptv/dot_general | solution.py:86
  79.0 2.8 %fusion.70 = f32[8,8,128,128]{3,1,2,0:T(8,128)} fusion(f32[8,8,128,128]{3,1,2,0:T(8,128)} %get-tuple-element.164, s32[]{:T(128)} %get-tuple-element.163, f32[32,128,128]{2,1,0:T(8,128)S(1)} %fusion.69, s32[32]{0:T(128)S(1)} %get-tuple-element.153, pred[32]{0:T(512)(128)(4,1)S(1)} %compare_bitcast_fusion.2), kind=kOutput, calls=%fused_computation.15.clone.1 | convolution fusion | flops 50332160 | bytes 2622112 | tf_op jit(solution)/shard_map/while/body/eval_jaxpr/rp,ptv->rtv/dot_general | solution.py:90
  81.8 6.1 %fusion.68 = f32[32,128,128]{2,0,1:T(8,128)S(1)} fusion(s32[32]{0:T(128)S(1)} %get-tuple-element.152, f32[8,8,128,128]{3,2,1,0:T(8,128)} %bitcast.92), kind=kOutput, calls=%fused_computation.2.clone.1 | convolution fusion | flops 402655232 | bytes 6291584 | tf_op jit(solution)/shard_map/while/body/eval_jaxpr/dot_general | solution.py:31
  87.9 5.0 %fusion.66 = f32[32,128,128]{2,0,1:T(8,128)S(1)} fusion(s32[32]{0:T(128)S(1)} %fusion.65, f32[6,8,128,128]{3,2,1,0:T(8,128)} %bitcast.89), kind=kOutput, calls=%fused_computation.6.clone.1 | convolution fusion | flops 301991424 | bytes 5243008 | tf_op jit(solution)/shard_map/while/body/eval_jaxpr/dot_general | solution.py:31
  92.9 4.6 %fusion.69 = f32[32,128,128]{2,1,0:T(8,128)S(1)} fusion(f32[32,128,128]{2,0,1:T(8,128)S(1)} %fusion.66, f32[32,128,128]{2,0,1:T(8,128)S(1)} %fusion.68), kind=kOutput, calls=%fused_computation.11.clone.1 | convolution fusion | flops 805306368 | bytes 6291456 | tf_op jit(solution)/shard_map/while/body/eval_jaxpr/ptu,puv->ptv/dot_general | solution.py:86
  97.5 2.8 %fusion.70 = f32[8,8,128,128]{3,1,2,0:T(8,128)} fusion(f32[8,8,128,128]{3,1,2,0:T(8,128)} %get-tuple-element.164, s32[]{:T(128)} %get-tuple-element.163, f32[32,128,128]{2,1,0:T(8,128)S(1)} %fusion.69, s32[32]{0:T(128)S(1)} %get-tuple-element.153, pred[32]{0:T(512)(128)(4,1)S(1)} %compare_bitcast_fusion.2), kind=kOutput, calls=%fused_computation.15.clone.1 | convolution fusion | flops 50332160 | bytes 2622112 | tf_op jit(solution)/shard_map/while/body/eval_jaxpr/rp,ptv->rtv/dot_general | solution.py:90
  100.3 6.1 %fusion.68 = f32[32,128,128]{2,0,1:T(8,128)S(1)} fusion(s32[32]{0:T(128)S(1)} %get-tuple-element.152, f32[8,8,128,128]{3,2,1,0:T(8,128)} %bitcast.92), kind=kOutput, calls=%fused_computation.2.clone.1 | convolution fusion | flops 402655232 | bytes 6291584 | tf_op jit(solution)/shard_map/while/body/eval_jaxpr/dot_general | solution.py:31
  106.3 5.0 %fusion.66 = f32[32,128,128]{2,0,1:T(8,128)S(1)} fusion(s32[32]{0:T(128)S(1)} %fusion.65, f32[6,8,128,128]{3,2,1,0:T(8,128)} %bitcast.89), kind=kOutput, calls=%fused_computation.6.clone.1 | convolution fusion | flops 301991424 | bytes 5243008 | tf_op jit(solution)/shard_map/while/body/eval_jaxpr/dot_general | solution.py:31
  111.4 4.6 %fusion.69 = f32[32,128,128]{2,1,0:T(8,128)S(1)} fusion(f32[32,128,128]{2,0,1:T(8,128)S(1)} %fusion.66, f32[32,128,128]{2,0,1:T(8,128)S(1)} %fusion.68), kind=kOutput, calls=%fused_computation.11.clone.1 | convolution fusion | flops 805306368 | bytes 6291456 | tf_op jit(solution)/shard_map/while/body/eval_jaxpr/ptu,puv->ptv/dot_general | solution.py:86
  116.0 2.8 %fusion.70 = f32[8,8,128,128]{3,1,2,0:T(8,128)} fusion(f32[8,8,128,128]{3,1,2,0:T(8,128)} %get-tuple-element.164, s32[]{:T(128)} %get-tuple-element.163, f32[32,128,128]{2,1,0:T(8,128)S(1)} %fusion.69, s32[32]{0:T(128)S(1)} %get-tuple-element.153, pred[32]{0:T(512)(128)(4,1)S(1)} %compare_bitcast_fusion.2), kind=kOutput, calls=%fused_computation.15.clone.1 | convolution fusion | flops 50332160 | bytes 2622112 | tf_op jit(solution)/shard_map/while/body/eval_jaxpr/rp,ptv->rtv/dot_general | solution.py:90
  118.8 6.1 %fusion.68 = f32[32,128,128]{2,0,1:T(8,128)S(1)} fusion(s32[32]{0:T(128)S(1)} %get-tuple-element.152, f32[8,8,128,128]{3,2,1,0:T(8,128)} %bitcast.92), kind=kOutput, calls=%fused_computation.2.clone.1 | convolution fusion | flops 402655232 | bytes 6291584 | tf_op jit(solution)/shard_map/while/body/eval_jaxpr/dot_general | solution.py:31
  124.8 5.0 %fusion.66 = f32[32,128,128]{2,0,1:T(8,128)S(1)} fusion(s32[32]{0:T(128)S(1)} %fusion.65, f32[6,8,128,128]{3,2,1,0:T(8,128)} %bitcast.89), kind=kOutput, calls=%fused_computation.6.clone.1 | convolution fusion | flops 301991424 | bytes 5243008 | tf_op jit(solution)/shard_map/while/body/eval_jaxpr/dot_general | solution.py:31
  129.9 4.6 %fusion.69 = f32[32,128,128]{2,1,0:T(8,128)S(1)} fusion(f32[32,128,128]{2,0,1:T(8,128)S(1)} %fusion.66, f32[32,128,128]{2,0,1:T(8,128)S(1)} %fusion.68), kind=kOutput, calls=%fused_computation.11.clone.1 | convolution fusion | flops 805306368 | bytes 6291456 | tf_op jit(solution)/shard_map/while/body/eval_jaxpr/ptu,puv->ptv/dot_general | solution.py:86
  134.5 2.8 %fusion.70 = f32[8,8,128,128]{3,1,2,0:T(8,128)} fusion(f32[8,8,128,128]{3,1,2,0:T(8,128)} %get-tuple-element.164, s32[]{:T(128)} %get-tuple-element.163, f32[32,128,128]{2,1,0:T(8,128)S(1)} %fusion.69, s32[32]{0:T(128)S(1)} %get-tuple-element.153, pred[32]{0:T(512)(128)(4,1)S(1)} %compare_bitcast_fusion.2), kind=kOutput, calls=%fused_computation.15.clone.1 | convolution fusion | flops 50332160 | bytes 2622112 | tf_op jit(solution)/shard_map/while/body/eval_jaxpr/rp,ptv->rtv/dot_general | solution.py:90
  137.2 6.1 %fusion.68 = f32[32,128,128]{2,0,1:T(8,128)S(1)} fusion(s32[32]{0:T(128)S(1)} %get-tuple-element.152, f32[8,8,128,128]{3,2,1,0:T(8,128)} %bitcast.92), kind=kOutput, calls=%fused_computation.2.clone.1 | convolution fusion | flops 402655232 | bytes 6291584 | tf_op jit(solution)/shard_map/while/body/eval_jaxpr/dot_general | solution.py:31
  143.3 5.0 %fusion.66 = f32[32,128,128]{2,0,1:T(8,128)S(1)} fusion(s32[32]{0:T(128)S(1)} %fusion.65, f32[6,8,128,128]{3,2,1,0:T(8,128)} %bitcast.89), kind=kOutput, calls=%fused_computation.6.clone.1 | convolution fusion | flops 301991424 | bytes 5243008 | tf_op jit(solution)/shard_map/while/body/eval_jaxpr/dot_general | solution.py:31
  148.3 4.6 %fusion.69 = f32[32,128,128]{2,1,0:T(8,128)S(1)} fusion(f32[32,128,128]{2,0,1:T(8,128)S(1)} %fusion.66, f32[32,128,128]{2,0,1:T(8,128)S(1)} %fusion.68), kind=kOutput, calls=%fused_computation.11.clone.1 | convolution fusion | flops 805306368 | bytes 6291456 | tf_op jit(solution)/shard_map/while/body/eval_jaxpr/ptu,puv->ptv/dot_general | solution.py:86
  152.9 2.8 %fusion.70 = f32[8,8,128,128]{3,1,2,0:T(8,128)} fusion(f32[8,8,128,128]{3,1,2,0:T(8,128)} %get-tuple-element.164, s32[]{:T(128)} %get-tuple-element.163, f32[32,128,128]{2,1,0:T(8,128)S(1)} %fusion.69, s32[32]{0:T(128)S(1)} %get-tuple-element.153, pred[32]{0:T(512)(128)(4,1)S(1)} %compare_bitcast_fusion.2), kind=kOutput, calls=%fused_computation.15.clone.1 | convolution fusion | flops 50332160 | bytes 2622112 | tf_op jit(solution)/shard_map/while/body/eval_jaxpr/rp,ptv->rtv/dot_general | solution.py:90
  155.7 6.1 %fusion.68 = f32[32,128,128]{2,0,1:T(8,128)S(1)} fusion(s32[32]{0:T(128)S(1)} %get-tuple-element.152, f32[8,8,128,128]{3,2,1,0:T(8,128)} %bitcast.92), kind=kOutput, calls=%fused_computation.2.clone.1 | convolution fusion | flops 402655232 | bytes 6291584 | tf_op jit(solution)/shard_map/while/body/eval_jaxpr/dot_general | solution.py:31
  161.8 5.0 %fusion.66 = f32[32,128,128]{2,0,1:T(8,128)S(1)} fusion(s32[32]{0:T(128)S(1)} %fusion.65, f32[6,8,128,128]{3,2,1,0:T(8,128)} %bitcast.89), kind=kOutput, calls=%fused_computation.6.clone.1 | convolution fusion | flops 301991424 | bytes 5243008 | tf_op jit(solution)/shard_map/while/body/eval_jaxpr/dot_general | solution.py:31
  166.8 4.6 %fusion.69 = f32[32,128,128]{2,1,0:T(8,128)S(1)} fusion(f32[32,128,128]{2,0,1:T(8,128)S(1)} %fusion.66, f32[32,128,128]{2,0,1:T(8,128)S(1)} %fusion.68), kind=kOutput, calls=%fused_computation.11.clone.1 | convolution fusion | flops 805306368 | bytes 6291456 | tf_op jit(solution)/shard_map/while/body/eval_jaxpr/ptu,puv->ptv/dot_general | solution.py:86
  171.4 2.8 %fusion.70 = f32[8,8,128,128]{3,1,2,0:T(8,128)} fusion(f32[8,8,128,128]{3,1,2,0:T(8,128)} %get-tuple-element.164, s32[]{:T(128)} %get-tuple-element.163, f32[32,128,128]{2,1,0:T(8,128)S(1)} %fusion.69, s32[32]{0:T(128)S(1)} %get-tuple-element.153, pred[32]{0:T(512)(128)(4,1)S(1)} %compare_bitcast_fusion.2), kind=kOutput, calls=%fused_computation.15.clone.1 | convolution fusion | flops 50332160 | bytes 2622112 | tf_op jit(solution)/shard_map/while/body/eval_jaxpr/rp,ptv->rtv/dot_general | solution.py:90
  174.2 6.1 %fusion.68 = f32[32,128,128]{2,0,1:T(8,128)S(1)} fusion(s32[32]{0:T(128)S(1)} %get-tuple-element.152, f32[8,8,128,128]{3,2,1,0:T(8,128)} %bitcast.92), kind=kOutput, calls=%fused_computation.2.clone.1 | convolution fusion | flops 402655232 | bytes 6291584 | tf_op jit(solution)/shard_map/while/body/eval_jaxpr/dot_general | solution.py:31
  180.3 5.0 %fusion.66 = f32[32,128,128]{2,0,1:T(8,128)S(1)} fusion(s32[32]{0:T(128)S(1)} %fusion.65, f32[6,8,128,128]{3,2,1,0:T(8,128)} %bitcast.89), kind=kOutput, calls=%fused_computation.6.clone.1 | convolution fusion | flops 301991424 | bytes 5243008 | tf_op jit(solution)/shard_map/while/body/eval_jaxpr/dot_general | solution.py:31
  185.3 4.6 %fusion.69 = f32[32,128,128]{2,1,0:T(8,128)S(1)} fusion(f32[32,128,128]{2,0,1:T(8,128)S(1)} %fusion.66, f32[32,128,128]{2,0,1:T(8,128)S(1)} %fusion.68), kind=kOutput, calls=%fused_computation.11.clone.1 | convolution fusion | flops 805306368 | bytes 6291456 | tf_op jit(solution)/shard_map/while/body/eval_jaxpr/ptu,puv->ptv/dot_general | solution.py:86
  189.9 2.8 %fusion.70 = f32[8,8,128,128]{3,1,2,0:T(8,128)} fusion(f32[8,8,128,128]{3,1,2,0:T(8,128)} %get-tuple-element.164, s32[]{:T(128)} %get-tuple-element.163, f32[32,128,128]{2,1,0:T(8,128)S(1)} %fusion.69, s32[32]{0:T(128)S(1)} %get-tuple-element.153, pred[32]{0:T(512)(128)(4,1)S(1)} %compare_bitcast_fusion.2), kind=kOutput, calls=%fused_computation.15.clone.1 | convolution fusion | flops 50332160 | bytes 2622112 | tf_op jit(solution)/shard_map/while/body/eval_jaxpr/rp,ptv->rtv/dot_general | solution.py:90
  192.7 6.1 %fusion.68 = f32[32,128,128]{2,0,1:T(8,128)S(1)} fusion(s32[32]{0:T(128)S(1)} %get-tuple-element.152, f32[8,8,128,128]{3,2,1,0:T(8,128)} %bitcast.92), kind=kOutput, calls=%fused_computation.2.clone.1 | convolution fusion | flops 402655232 | bytes 6291584 | tf_op jit(solution)/shard_map/while/body/eval_jaxpr/dot_general | solution.py:31
  198.7 5.0 %fusion.66 = f32[32,128,128]{2,0,1:T(8,128)S(1)} fusion(s32[32]{0:T(128)S(1)} %fusion.65, f32[6,8,128,128]{3,2,1,0:T(8,128)} %bitcast.89), kind=kOutput, calls=%fused_computation.6.clone.1 | convolution fusion | flops 301991424 | bytes 5243008 | tf_op jit(solution)/shard_map/while/body/eval_jaxpr/dot_general | solution.py:31
  203.8 4.6 %fusion.69 = f32[32,128,128]{2,1,0:T(8,128)S(1)} fusion(f32[32,128,128]{2,0,1:T(8,128)S(1)} %fusion.66, f32[32,128,128]{2,0,1:T(8,128)S(1)} %fusion.68), kind=kOutput, calls=%fused_computation.11.clone.1 | convolution fusion | flops 805306368 | bytes 6291456 | tf_op jit(solution)/shard_map/while/body/eval_jaxpr/ptu,puv->ptv/dot_general | solution.py:86
  208.4 2.8 %fusion.70 = f32[8,8,128,128]{3,1,2,0:T(8,128)} fusion(f32[8,8,128,128]{3,1,2,0:T(8,128)} %get-tuple-element.164, s32[]{:T(128)} %get-tuple-element.163, f32[32,128,128]{2,1,0:T(8,128)S(1)} %fusion.69, s32[32]{0:T(128)S(1)} %get-tuple-element.153, pred[32]{0:T(512)(128)(4,1)S(1)} %compare_bitcast_fusion.2), kind=kOutput, calls=%fused_computation.15.clone.1 | convolution fusion | flops 50332160 | bytes 2622112 | tf_op jit(solution)/shard_map/while/body/eval_jaxpr/rp,ptv->rtv/dot_general | solution.py:90
  211.1 53.5 %all_to_all.10 = f32[8,8,128,128]{3,1,2,0:T(8,128)} all-to-all(f32[8,8,128,128]{3,1,2,0:T(8,128)} %get-tuple-element.52), channel_id=1, replica_groups=mesh['rows'=8,'blk'=4] {'rows'}, dimensions={0} | all-to-all | bytes 8388608 | tf_op jit(solution)/shard_map/all_to_all | solution.py:93
  264.7 2.5 reduce_sum.59
  267.2 1.5 fusion.33
  (43 shorter events, 0.3 us)
Async XLA Ops:
  0.0 1.1 copy-start
  0.0 3.2 %copy-start.1 = (f32[12,128,128]{2,1,0:T(8,128)S(1)}, f32[12,128,128]{2,1,0:T(8,128)}, u32[]{:S(2)}) copy-start(f32[12,128,128]{2,1,0:T(8,128)} %param.12) | copy-start | bytes 2359300
  1.1 9.7 %copy-start.3 = (s32[8,32]{1,0:T(8,128)S(1)}, s32[8,32]{1,0:T(8,128)}, u32[]{:S(2)}) copy-start(s32[8,32]{1,0:T(8,128)} %param.15) | copy-start | bytes 3076
  1.1 9.8 %copy-start.6 = (s32[8]{0:T(128)S(1)}, s32[8]{0:T(128)}, u32[]{:S(2)}) copy-start(s32[8]{0:T(128)} %param.17) | copy-start | bytes 100
  1.1 28.4 %copy-start.4 = (s32[8,32]{1,0:T(8,128)S(1)}, s32[8,32]{1,0:T(8,128)}, u32[]{:S(2)}) copy-start(s32[8,32]{1,0:T(8,128)} %param.16) | copy-start | bytes 3076
  1.1 28.5 %copy-start.5 = (s32[8,32]{1,0:T(8,128)S(1)}, s32[8,32]{1,0:T(8,128)}, u32[]{:S(2)}) copy-start(s32[8,32]{1,0:T(8,128)} %param.14) | copy-start | bytes 3076
  5.8 23.7 %collective-permute-start = (f32[12,128,128]{2,1,0:T(8,128)}, f32[12,128,128]{2,1,0:T(8,128)S(1)}, u32[]{:S(2)}, u32[]{:S(2)}) collective-permute-start(f32[12,128,128]{2,1,0:T(8,128)} %get-tuple-element.98), channel_id=1, source_target_pairs={{0,1},{1,2},{2,3},{3,0},{4,5},{5,6},{6,7},{7,4},{8,9},{9,10},{10,1... | collective-permute-start | bytes 2359304 | tf_op jit(solution)/shard_map/ppermute | solution.py:16
  8.9 36.3 %collective-permute-start.1 = (f32[12,128,128]{2,1,0:T(8,128)}, f32[12,128,128]{2,1,0:T(8,128)S(1)}, u32[]{:S(2)}, u32[]{:S(2)}) collective-permute-start(f32[12,128,128]{2,1,0:T(8,128)} %get-tuple-element.98), channel_id=1, source_target_pairs={{0,3},{1,0},{2,1},{3,2},{4,7},{5,4},{6,5},{7,6},{8,11},{9,8},{10,9... | collective-permute-start | bytes 2359304 | tf_op jit(solution)/shard_map/ppermute | solution.py:21
  29.5 32.9 %collective-permute-start.2 = (f32[12,128,128]{2,1,0:T(8,128)S(1)}, f32[12,128,128]{2,1,0:T(8,128)S(1)}, u32[]{:S(2)}, u32[]{:S(2)}) collective-permute-start(f32[12,128,128]{2,1,0:T(8,128)S(1)} %collective-permute-done), channel_id=1, source_target_pairs={{0,1},{1,2},{2,3},{3,0},{4,5},{5,6},{6,7},{7,4},{8,9},{9,10},{10,1... | collective-permute-start | bytes 2359304 | tf_op jit(solution)/shard_map/ppermute | solution.py:16
  31.0 8.6 %all-to-all-start = ((s32[8,1,128]{2,1,0:T(1,128)}), s32[8,1,128]{2,1,0:T(1,128)S(1)}, u32[]{:S(2)}, u32[]{:S(2)}) async-start(s32[8,1,128]{2,1,0:T(1,128)} %reshape.85), calls=%async_computation | async-start | bytes 8192 | tf_op jit(solution)/shard_map/all_to_all | solution.py:77
  264.7 2.5 copy-start.2
